TPU v7x, 32 devices: a whole 2x2x4 slice. The times are simulated.
32 devices in a mesh: dp: 8 (over z, y), fsdp: 4 (over x, core).
Axes of the slice: x: 2, y: 2, z: 4, core: 2. Of those that a mesh axis runs over, the one named last changes fastest.
Arguments:
- tokens: bfloat16 [1536, 16, 768], P(('dp', 'fsdp')), may hold values from -6 to 6
- image_embed: bfloat16 [1536, 768], P(('dp', 'fsdp')), may hold values from -6 to 6
- counts: int32 [32], replicated, may hold values from 12 to 48, as said below
- end_pos: int32 [1536], P(('dp', 'fsdp')), may hold values from 2 to 15
- ln1_gain: bfloat16 [768], P(('dp', 'fsdp')), may hold values from 0.5 to 1.5
- ln1_bias: bfloat16 [768], P(('dp', 'fsdp')), may hold values from -1.1953125 to 1.1953125
- w_qkv: bfloat16 [768, 2304], P(('dp', 'fsdp')), may hold values from -0.21875 to 0.21875
- w_out: bfloat16 [768, 768], P(('dp', 'fsdp')), may hold values from -0.625 to 0.625
- ln2_gain: bfloat16 [768], P(('dp', 'fsdp')), may hold values from 0.5 to 1.5
- ln2_bias: bfloat16 [768], P(('dp', 'fsdp')), may hold values from -1.1953125 to 1.1953125
- w_up: bfloat16 [768, 3072], P(('dp', 'fsdp')), may hold values from -0.21875 to 0.21875
- b_up: bfloat16 [3072], P(('dp', 'fsdp')), may hold values from -1.1953125 to 1.1953125
- w_down: bfloat16 [3072, 768], P(('dp', 'fsdp')), may hold values from -0.109375 to 0.109375
- b_down: bfloat16 [768], P(('dp', 'fsdp')), may hold values from -1.1953125 to 1.1953125
Outputs:
- mean_loss: float32 [], replicated
- grad_tokens: float32 [1536, 16, 768], P(('dp', 'fsdp'))
- grad_ln1_gain: float32 [768], P(('dp', 'fsdp'))
- grad_ln1_bias: float32 [768], P(('dp', 'fsdp'))
- grad_w_qkv: float32 [768, 2304], P(('dp', 'fsdp'))
- grad_w_out: float32 [768, 768], P(('dp', 'fsdp'))
- grad_ln2_gain: float32 [768], P(('dp', 'fsdp'))
- grad_ln2_bias: float32 [768], P(('dp', 'fsdp'))
- grad_w_up: float32 [768, 3072], P(('dp', 'fsdp'))
- grad_b_up: float32 [3072], P(('dp', 'fsdp'))
- grad_w_down: float32 [3072, 768], P(('dp', 'fsdp'))
- grad_b_down: float32 [768], P(('dp', 'fsdp'))
Inputs may be any that keep to these rules, and one draw needn't show every extreme that they name: counts[r] valid captions occupy the first counts[r] of the 48 slots of device r; some device is full in every draw. Slots 0 to end_pos of a caption are its tokens.
All inputs are finite; a program needn't handle non-finite values.
Results may differ from a plain program's by a relative error of at most 0.0109.
Values may be sent and summed in bfloat16 or wider, within the bound.
A program may use at most 192 MiB of HBM per device.

v0:
```python
import jax
import jax.numpy as jnp
from jax import lax
from jax.sharding import PartitionSpec as P

HEAD_DIM = 64


EPS = 1e-05
NORM_EPS = 1e-06
SCALE = 50.0
NEG = -1e30


def layer_norm(values, gain_vec, shift_vec):
    average = jnp.mean(values, axis=-1, keepdims=True)
    centred = values - average
    variance = jnp.mean(centred * centred, axis=-1, keepdims=True)
    return centred * lax.rsqrt(variance + EPS) * gain_vec + shift_vec


def unit_rows(values):
    return values * lax.rsqrt(jnp.sum(values * values, axis=-1, keepdims=True) + NORM_EPS)


def gelu_exact(values):
    return jax.nn.gelu(values, approximate=False)


def validity(counts, row_start, number, per_dev):
    row_index = row_start + jnp.arange(number, dtype=jnp.int32)
    owner_dev = row_index // per_dev
    within = row_index % per_dev
    rank_ids = jnp.arange(counts.shape[0], dtype=jnp.int32)
    limit_rows = jnp.sum(
        jnp.where(owner_dev[:, None] == rank_ids[None, :], counts[None, :], 0), axis=1
    )
    return (within < limit_rows).astype(jnp.float32)


def scores_of(left_rows, right_rows):
    return SCALE * lax.dot_general(
        left_rows, right_rows, (((1,), (1,)), ((), ())), preferred_element_type=jnp.float32
    )


def merge_scores(running, scores, column_ok):
    top_prev, total_prev = running
    masked = jnp.where(column_ok[None, :] > 0, scores, NEG)
    top_new = jnp.maximum(top_prev, jnp.max(masked, axis=1))
    exp_terms = jnp.where(column_ok[None, :] > 0, jnp.exp(masked - top_new[:, None]), 0.0)
    return (top_new, jnp.sum(exp_terms, axis=1))


def masked_scores(queries, keys_all, key_ok):
    raw_scores = jnp.einsum(
        "cqhe,ckhe->chqk", queries, keys_all, preferred_element_type=jnp.float32
    ) * HEAD_DIM ** (-0.5)
    return jnp.where(key_ok[:, None, None, :], raw_scores, NEG)


def on_device(
    tokens,
    image_embed,
    counts,
    end_pos,
    ln1_gain,
    ln1_bias,
    w_qkv,
    w_out,
    ln2_gain,
    ln2_bias,
    w_up,
    b_up,
    w_down,
    b_down,
):
    cap_count, seq_len, model_dim = tokens.shape
    head_count = model_dim // HEAD_DIM
    tok_rows = cap_count * seq_len
    own_start = lax.axis_index(("dp", "fsdp")) * cap_count
    attn_full = (
        lax.all_gather(ln1_gain, ("dp", "fsdp"), axis=0, tiled=True),
        lax.all_gather(ln1_bias, ("dp", "fsdp"), axis=0, tiled=True),
        lax.all_gather(w_qkv, ("dp", "fsdp"), axis=0, tiled=True),
        lax.all_gather(w_out, ("dp", "fsdp"), axis=0, tiled=True),
    )
    gain_one, shift_one, wqkv_all, wout_all = attn_full
    inputs = tokens.reshape(tok_rows, model_dim).astype(jnp.float32)
    normed, norm1_back = jax.vjp(
        layer_norm, inputs, gain_one.astype(jnp.float32), shift_one.astype(jnp.float32)
    )
    normed_low = normed.astype(jnp.bfloat16)
    qkv_low = jnp.dot(normed_low, wqkv_all, preferred_element_type=jnp.float32).astype(jnp.bfloat16)
    split_qkv = qkv_low.reshape(cap_count, seq_len, 3, head_count, HEAD_DIM)
    queries = split_qkv[:, :, 0]
    keys_all = split_qkv[:, :, 1]
    values_all = split_qkv[:, :, 2]
    positions = jnp.arange(seq_len, dtype=jnp.int32)
    key_ok = positions[None, :] <= end_pos[:, None]
    masked_one = masked_scores(queries, keys_all, key_ok)
    top_one = jnp.max(masked_one, axis=-1, keepdims=True)
    lse_heads = top_one + jnp.log(jnp.sum(jnp.exp(masked_one - top_one), axis=-1, keepdims=True))
    probs_low = jnp.exp(masked_one - lse_heads).astype(jnp.bfloat16)
    mixed_heads = jnp.einsum(
        "chqk,ckhe->cqhe", probs_low, values_all, preferred_element_type=jnp.float32
    )
    mixed_low = mixed_heads.reshape(tok_rows, model_dim).astype(jnp.bfloat16)
    hidden_one = inputs + jnp.dot(mixed_low, wout_all, preferred_element_type=jnp.float32)
    mlp_full = (
        lax.all_gather(ln2_gain, ("dp", "fsdp"), axis=0, tiled=True),
        lax.all_gather(ln2_bias, ("dp", "fsdp"), axis=0, tiled=True),
        lax.all_gather(w_up, ("dp", "fsdp"), axis=0, tiled=True),
        lax.all_gather(b_up, ("dp", "fsdp"), axis=0, tiled=True),
        lax.all_gather(w_down, ("dp", "fsdp"), axis=0, tiled=True),
        lax.all_gather(b_down, ("dp", "fsdp"), axis=0, tiled=True),
    )
    gain_two, shift_two, wup_all, bup_all, wdown_all, bdown_all = mlp_full
    normed_two, norm2_back = jax.vjp(
        layer_norm, hidden_one, gain_two.astype(jnp.float32), shift_two.astype(jnp.float32)
    )
    normed2_low = normed_two.astype(jnp.bfloat16)
    upper_pre = jnp.dot(normed2_low, wup_all, preferred_element_type=jnp.float32) + bup_all.astype(
        jnp.float32
    )
    acted_val, gelu_back = jax.vjp(gelu_exact, upper_pre)
    acted_low = acted_val.astype(jnp.bfloat16)
    hidden_two = hidden_one + (
        jnp.dot(acted_low, wdown_all, preferred_element_type=jnp.float32)
        + bdown_all.astype(jnp.float32)
    )
    end_pick = (positions[None, :] == end_pos[:, None]).astype(jnp.float32)
    pooled = jnp.sum(
        hidden_two.reshape(cap_count, seq_len, model_dim) * end_pick[:, :, None], axis=1
    )
    text_unit, unit_back = jax.vjp(unit_rows, pooled)
    text_low = text_unit.astype(jnp.bfloat16)
    image_low = unit_rows(image_embed.astype(jnp.float32)).astype(jnp.bfloat16)
    own_valid = validity(counts, own_start, cap_count, cap_count)
    diagonal = SCALE * jnp.sum(text_low.astype(jnp.float32) * image_low.astype(jnp.float32), axis=1)
    text_group, image_group = (
        lax.all_gather(text_low, "fsdp", axis=0, tiled=True),
        lax.all_gather(image_low, "fsdp", axis=0, tiled=True),
    )
    start_state = (jnp.full((cap_count,), NEG, jnp.float32), jnp.zeros((cap_count,), jnp.float32))
    image_piece = lax.all_gather(image_group, "dp", axis=0, tiled=True)
    text_piece = lax.all_gather(text_group, "dp", axis=0, tiled=True)
    column_ok = validity(counts, jnp.int32(0), image_piece.shape[0], cap_count)
    row_next = merge_scores(start_state, scores_of(text_low, image_piece), column_ok)
    col_next = merge_scores(start_state, scores_of(image_low, text_piece), column_ok)
    row_lse = row_next[0] + jnp.log(row_next[1])
    col_lse = col_next[0] + jnp.log(col_next[1])
    local_part = 0.5 * jnp.sum(own_valid * (row_lse - diagonal)) + 0.5 * jnp.sum(
        own_valid * (col_lse - diagonal)
    )
    objective = lax.psum(local_part, ("dp", "fsdp"))
    mean_loss = objective / jnp.sum(counts).astype(jnp.float32)
    col_all = lax.all_gather(col_lse, ("dp", "fsdp"), axis=0, tiled=True)
    image_piece = lax.all_gather(image_group, "dp", axis=0, tiled=True)
    number = image_piece.shape[0]
    column_ok = validity(counts, jnp.int32(0), number, cap_count)
    scores = scores_of(text_low, image_piece)
    pair_ok = own_valid[:, None] * column_ok[None, :] > 0
    weight = jnp.where(
        pair_ok, jnp.exp(scores - row_lse[:, None]) + jnp.exp(scores - col_all[None, :]), 0.0
    )
    coef_low = (0.5 * SCALE * weight).astype(jnp.bfloat16)
    dt_pairs = jnp.dot(coef_low, image_piece, preferred_element_type=jnp.float32)
    d_text = dt_pairs - SCALE * own_valid[:, None] * image_low.astype(jnp.float32)
    d_pooled = unit_back(d_text)[0]
    d_hidden2 = (end_pick[:, :, None] * d_pooled[:, None, :]).reshape(tok_rows, model_dim)
    attn_back = (
        lax.all_gather(ln1_gain, ("dp", "fsdp"), axis=0, tiled=True),
        lax.all_gather(ln1_bias, ("dp", "fsdp"), axis=0, tiled=True),
        lax.all_gather(w_qkv, ("dp", "fsdp"), axis=0, tiled=True),
        lax.all_gather(w_out, ("dp", "fsdp"), axis=0, tiled=True),
    )
    mlp_back = (
        lax.all_gather(ln2_gain, ("dp", "fsdp"), axis=0, tiled=True),
        lax.all_gather(ln2_bias, ("dp", "fsdp"), axis=0, tiled=True),
        lax.all_gather(w_up, ("dp", "fsdp"), axis=0, tiled=True),
        lax.all_gather(b_up, ("dp", "fsdp"), axis=0, tiled=True),
        lax.all_gather(w_down, ("dp", "fsdp"), axis=0, tiled=True),
        lax.all_gather(b_down, ("dp", "fsdp"), axis=0, tiled=True),
    )
    wqkv_back = attn_back[2]
    wout_back = attn_back[3]
    wup_back = mlp_back[2]
    wdown_back = mlp_back[4]
    d_out_low = d_hidden2.astype(jnp.bfloat16)
    grad_wdown = jnp.einsum("rf,rd->fd", acted_low, d_out_low, preferred_element_type=jnp.float32)
    grad_bdown = jnp.sum(d_out_low.astype(jnp.float32), axis=0)
    d_acted = jnp.einsum("rd,fd->rf", d_out_low, wdown_back, preferred_element_type=jnp.float32)
    d_upper = gelu_back(d_acted)[0].astype(jnp.bfloat16)
    grad_bup = jnp.sum(d_upper.astype(jnp.float32), axis=0)
    grad_wup = jnp.einsum("rd,rf->df", normed2_low, d_upper, preferred_element_type=jnp.float32)
    d_normed2 = jnp.einsum("rf,df->rd", d_upper, wup_back, preferred_element_type=jnp.float32)
    d_hid_part, grad_gain2, grad_shift2 = norm2_back(d_normed2)
    d_hidden1 = d_hidden2 + d_hid_part
    mlp_grads = (
        lax.psum_scatter(grad_gain2, ("dp", "fsdp"), scatter_dimension=0, tiled=True),
        lax.psum_scatter(grad_shift2, ("dp", "fsdp"), scatter_dimension=0, tiled=True),
        lax.psum_scatter(grad_wup, ("dp", "fsdp"), scatter_dimension=0, tiled=True),
        lax.psum_scatter(grad_bup, ("dp", "fsdp"), scatter_dimension=0, tiled=True),
        lax.psum_scatter(grad_wdown, ("dp", "fsdp"), scatter_dimension=0, tiled=True),
        lax.psum_scatter(grad_bdown, ("dp", "fsdp"), scatter_dimension=0, tiled=True),
    )
    d_branch_low = d_hidden1.astype(jnp.bfloat16)
    grad_wout = jnp.einsum("rd,re->de", mixed_low, d_branch_low, preferred_element_type=jnp.float32)
    d_mixed = jnp.einsum(
        "re,de->rd", d_branch_low, wout_back, preferred_element_type=jnp.float32
    ).astype(jnp.bfloat16)
    d_mixed = d_mixed.reshape(cap_count, seq_len, head_count, HEAD_DIM)
    probs_again = jnp.exp(masked_scores(queries, keys_all, key_ok) - lse_heads)
    d_values = jnp.einsum(
        "chqk,cqhe->ckhe",
        probs_again.astype(jnp.bfloat16),
        d_mixed,
        preferred_element_type=jnp.float32,
    )
    d_probs = jnp.einsum("cqhe,ckhe->chqk", d_mixed, values_all, preferred_element_type=jnp.float32)
    d_raw = (
        probs_again * (d_probs - jnp.sum(d_probs * probs_again, axis=-1, keepdims=True))
    ).astype(jnp.bfloat16)
    attn_scale = HEAD_DIM ** (-0.5)
    d_queries = attn_scale * jnp.einsum(
        "chqk,ckhe->cqhe", d_raw, keys_all, preferred_element_type=jnp.float32
    )
    d_keys = attn_scale * jnp.einsum(
        "chqk,cqhe->ckhe", d_raw, queries, preferred_element_type=jnp.float32
    )
    d_qkv = (
        jnp.stack([d_queries, d_keys, d_values], axis=2)
        .reshape(tok_rows, 3 * model_dim)
        .astype(jnp.bfloat16)
    )
    grad_wqkv = jnp.einsum("rd,re->de", normed_low, d_qkv, preferred_element_type=jnp.float32)
    d_normed = jnp.einsum("re,de->rd", d_qkv, wqkv_back, preferred_element_type=jnp.float32)
    d_in_part, grad_gain1, grad_shift1 = norm1_back(d_normed)
    grad_input = (d_hidden1 + d_in_part).reshape(cap_count, seq_len, model_dim)
    attn_grads = (
        lax.psum_scatter(grad_gain1, ("dp", "fsdp"), scatter_dimension=0, tiled=True),
        lax.psum_scatter(grad_shift1, ("dp", "fsdp"), scatter_dimension=0, tiled=True),
        lax.psum_scatter(grad_wqkv, ("dp", "fsdp"), scatter_dimension=0, tiled=True),
        lax.psum_scatter(grad_wout, ("dp", "fsdp"), scatter_dimension=0, tiled=True),
    )
    return (
        mean_loss,
        grad_input,
        attn_grads[0],
        attn_grads[1],
        attn_grads[2],
        attn_grads[3],
        mlp_grads[0],
        mlp_grads[1],
        mlp_grads[2],
        mlp_grads[3],
        mlp_grads[4],
        mlp_grads[5],
    )


def solution(mesh):
    placed = (
        P(("dp", "fsdp"), None, None),
        P(("dp", "fsdp"), None),
        P(),
        P(("dp", "fsdp")),
        P(("dp", "fsdp")),
        P(("dp", "fsdp")),
        P(("dp", "fsdp"), None),
        P(("dp", "fsdp"), None),
        P(("dp", "fsdp")),
        P(("dp", "fsdp")),
        P(("dp", "fsdp"), None),
        P(("dp", "fsdp")),
        P(("dp", "fsdp"), None),
        P(("dp", "fsdp")),
    )
    return jax.shard_map(
        on_device,
        mesh=mesh,
        in_specs=placed,
        out_specs=(
            P(),
            P(("dp", "fsdp"), None, None),
            P(("dp", "fsdp")),
            P(("dp", "fsdp")),
            P(("dp", "fsdp"), None),
            P(("dp", "fsdp"), None),
            P(("dp", "fsdp")),
            P(("dp", "fsdp")),
            P(("dp", "fsdp"), None),
            P(("dp", "fsdp")),
            P(("dp", "fsdp"), None),
            P(("dp", "fsdp")),
        ),
        check_vma=False,
    )
```

profile of v0, /device:TPU:0, one launch (start us, length us, event | category | flops | bytes accessed | tf_op | source)
XLA Modules:
  0.0 991.7 jit_solution(3140025889975995914)
XLA Ops:
  18.4 42.7 %all-reduce.14 = (bf16[768]{0:T(1024)(128)(2,1)S(1)}, bf16[768]{0:T(1024)(128)(2,1)S(1)}, bf16[768]{0:T(1024)(128)(2,1)S(1)}, bf16[768]{0:T(1024)(128)(2,1)S(1)}...) all-reduce(bf16[768]{0:T(1024)(128)(2,1)S(1)} %dynamic-update-slice, ...), channel_id=1, replica_groups=mesh['dp'=8,'fsdp'=4] {'dp','fsdp'}, use_global_device_ids=true, to_apply=%add.1 | all-reduce | flops 6912 | bytes 27648
  65.6 8.4 all-gather.7.cloned.1.call-done
  80.4 11.6 %reshape.309 = bf16[48,16,3,12,64]{4,3,2,1,0:T(8,128)(2,1)} reshape(bf16[768,2304]{1,0:T(8,128)(2,1)} %convolution_convert_fusion) | data formatting | bytes 7077888 | tf_op jit(solution)/shard_map/reshape | solution.py:95
  111.0 18.8 %all-gather.9.cloned.1.call-done = bf16[768,768]{1,0:T(8,128)(2,1)} async-done(((bf16[24,768]{1,0:T(8,128)(2,1)}), bf16[768,768]{1,0:T(8,128)(2,1)}) %all-gather.9.cloned.1.call-update) | async-done | bytes 1179664 | tf_op jit(solution)/shard_map/all_gather | solution.py:86
  133.9 61.4 %all-gather.11.cloned.1.call-done = bf16[768,3072]{1,0:T(8,128)(2,1)} async-done(((bf16[24,3072]{1,0:T(8,128)(2,1)}), bf16[768,3072]{1,0:T(8,128)(2,1)}) %all-gather.11.cloned.1.call-update) | async-done | bytes 4718608 | tf_op jit(solution)/shard_map/all_gather | solution.py:113
  195.3 28.0 %multiply_convert_fusion = (bf16[768,3072]{1,0:T(8,128)(2,1)}, f32[768,3072]{1,0:T(8,128)}, f32[768,3072]{1,0:T(8,128)}) fusion(f32[3072]{0:T(1024)} %convert_element_type.166, bf16[768,3072]{1,0:T(8,128)(2,1)} %all-gather.11.cloned.1.call-done, f32[768,768]{1,0:T(8,128)S(1)} %get-tuple-element.61, f32[768]{0:T(1024)S(1)} %convert_element_type.164, ...), kind=kOutput, calls=%fused_computation.5 | convolution fusion | flops 3782541312 | bytes 30695424 | tf_op jit(solution)/shard_map/dot_general | solution.py:123
  223.3 37.2 %all-gather.13.cloned.1.call-done = bf16[3072,768]{1,0:T(8,128)(2,1)} async-done(((bf16[96,768]{1,0:T(8,128)(2,1)}), bf16[3072,768]{1,0:T(8,128)(2,1)}) %all-gather.13.cloned.1.call-update) | async-done | bytes 4718608 | tf_op jit(solution)/shard_map/all_gather | solution.py:115
  260.5 7.1 add_add_fusion.3
  277.3 7.9 all_gather.60
  292.1 36.2 %all-gather.17.cloned.1.call-done = bf16[1536,768]{1,0:T(8,128)(2,1)} async-done(((bf16[192,768]{1,0:T(8,128)(2,1)}), bf16[1536,768]{1,0:T(8,128)(2,1)}) %all-gather.17.cloned.1.call-update) | async-done | bytes 2359312 | tf_op jit(solution)/shard_map/all_gather | solution.py:147
  332.7 48.4 %all-gather.15.cloned.1.call-done = bf16[1536,768]{1,0:T(8,128)(2,1)} async-done(((bf16[192,768]{1,0:T(8,128)(2,1)}), bf16[1536,768]{1,0:T(8,128)(2,1)}) %all-gather.15.cloned.1.call-update) | async-done | bytes 2359312 | tf_op jit(solution)/shard_map/all_gather | solution.py:146
  388.2 39.9 %all-reduce.6 = f32[1536]{0:T(1024)} all-reduce(f32[1536]{0:T(1024)} %get-tuple-element.55), channel_id=1, replica_groups=mesh['dp'=8,'fsdp'=4] {'dp','fsdp'}, use_global_device_ids=true, to_apply=%add.6 | all-reduce | flops 1536 | bytes 12288
  432.3 12.8 %convert_reduce_fusion = (f32[3072]{0:T(1024)}, bf16[768,3072]{1,0:T(8,128)(2,1)S(1)}) fusion(f32[768,3072]{1,0:T(8,128)} %get-tuple-element.47, f32[768,3072]{1,0:T(8,128)} %get-tuple-element.62, f32[3072]{0:T(1024)S(1)} %copy-done.42, bf16[768,768]{1,0:T(8,128)(2,1)S(1)} %fusion.9, bf16[3072,768]{1,0:T(8,128)(2,1)} %all-gather.13.cloned.1.call-done), kind=kOutput, calls=%fused_computation.3 | convolution fusion | flops 3663983616 | bytes 29515776 | tf_op jit(solution)/shard_map/rd,fd->rf/dot_general | solution.py:193
  465.4 9.5 multiply_reduce_fusion
  489.8 9.2 copy.59
  499.0 12.0 %convert_element_type.186 = bf16[768,2304]{1,0:T(8,128)(2,1)} reshape(bf16[48,16,3,12,64]{4,3,2,1,0:T(8,128)(2,1)} %copy.59) | data formatting | bytes 7077888 | tf_op jit(solution)/shard_map/convert_element_type | solution.py:235
  511.0 8.3 fusion.68
  519.6 10.9 %fusion.58 = f32[768,3072]{1,0:T(8,128)} fusion(bf16[768,3072]{1,0:T(8,128)(2,1)} %copy-done.12, f32[768,768]{1,0:T(8,128)} %copy-done.2, f32[768]{0:T(1024)S(1)} %convert_element_type.164, f32[768]{0:T(1024)S(1)} %convert_element_type.163, f32[768]{0:T(1024)S(1)} %fusion.48, f32[768]{0:T(1024)S(1)} %broadcast_multiply_fusion.1), kind=kOutput, calls=%fused_computation.149 | convolution fusion | flops 3626827776 | bytes 16527360 | tf_op jit(solution)/shard_map/rd,rf->df/dot_general | solution.py:196
  530.5 10.3 %fusion.70 = f32[3072,768]{1,0:T(8,128)} fusion(bf16[768,3072]{1,0:T(8,128)(2,1)} %get-tuple-element.46, bf16[768,768]{1,0:T(8,128)(2,1)} %copy-done.18), kind=kOutput, calls=%fused_computation.158 | convolution fusion | flops 3623878656 | bytes 15335424 | tf_op jit(solution)/shard_map/rf,rd->fd/dot_general | solution.py:191
  545.8 6.8 fusion.60
  555.8 41.9 %all-reduce.13 = (f32[]{:T(128)}, f32[768]{0:T(1024)}, f32[768]{0:T(1024)}, f32[768]{0:T(1024)}, f32[768]{0:T(1024)}, /*index=5*/f32[3072]{0:T(1024)}, f32[768]{0:T(1024)}) all-reduce(f32[]{:T(128)S(6)} %add.218, f32[768]{0:T(1024)} %get-tuple-element.14, ...), channel_id=1, replica_groups=mesh['dp'=8,'fsdp'=4] {'dp','fsdp'}, use_global_device_ids=true, to_apply=%region_18.19 | all-reduce | flops 6913 | bytes 55304 | tf_op jit(solution)/shard_map/psum | solution.py:156
  611.3 88.8 %reduce-scatter.5.cloned.1.call-done = f32[24,2304]{1,0:T(8,128)} async-done(((f32[768,2304]{1,0:T(8,128)}), f32[24,2304]{1,0:T(8,128)}) %reduce-scatter.5.cloned.1.call-update) | async-done | bytes 221200 | tf_op jit(solution)/shard_map/reduce_scatter | solution.py:244
  700.1 141.5 %reduce-scatter.9.cloned.1.call-done = f32[24,3072]{1,0:T(8,128)} async-done(((f32[768,3072]{1,0:T(8,128)}), f32[24,3072]{1,0:T(8,128)}) %reduce-scatter.9.cloned.1.call-update) | async-done | bytes 294928 | tf_op jit(solution)/shard_map/reduce_scatter | solution.py:203
  841.5 142.0 %reduce-scatter.11.cloned.1.call-done = f32[96,768]{1,0:T(8,128)} async-done(((f32[3072,768]{1,0:T(8,128)}), f32[96,768]{1,0:T(8,128)}) %reduce-scatter.11.cloned.1.call-update) | async-done | bytes 294928 | tf_op jit(solution)/shard_map/reduce_scatter | solution.py:205
  (225 shorter events, 131.5 us)
Async XLA Ops:
  7.2 57.9 %copy-start.1 = (bf16[48,16,768]{2,1,0:T(8,128)(2,1)S(1)}, bf16[48,16,768]{2,1,0:T(8,128)(2,1)}, u32[]{:S(2)}) copy-start(bf16[48,16,768]{2,1,0:T(8,128)(2,1)} %param.14) | copy-start | bytes 3538948
  7.2 57.2 %copy-start.23 = (bf16[48,768]{1,0:T(8,128)(2,1)S(1)}, bf16[48,768]{1,0:T(8,128)(2,1)}, u32[]{:S(2)}) copy-start(bf16[48,768]{1,0:T(8,128)(2,1)} %param.15) | copy-start | bytes 221188
  7.2 66.8 %all-gather.7.cloned.1.call-start = ((), (), s32[]{:S(2)}) async-start(), calls=%async_computation.4 | async-start | bytes 3649536 | tf_op jit(solution)/shard_map/all_gather | solution.py:85
  7.9 121.8 %all-gather.9.cloned.1.call-start = ((), (), s32[]{:S(2)}) async-start(), calls=%async_computation.5 | async-start | bytes 1216512 | tf_op jit(solution)/shard_map/all_gather | solution.py:86
  8.7 186.6 %all-gather.11.cloned.1.call-start = ((), (), s32[]{:S(2)}) async-start(), calls=%async_computation.6 | async-start | bytes 4866048 | tf_op jit(solution)/shard_map/all_gather | solution.py:113
  9.4 251.1 %all-gather.13.cloned.1.call-start = ((), (), s32[]{:S(2)}) async-start(), calls=%async_computation.7 | async-start | bytes 4866048 | tf_op jit(solution)/shard_map/all_gather | solution.py:115
  10.0 318.3 %all-gather.17.cloned.1.call-start = ((), (), s32[]{:S(2)}) async-start(), calls=%async_computation.9 | async-start | bytes 2654208 | tf_op jit(solution)/shard_map/all_gather | solution.py:147
  11.6 52.9 %copy-start.22 = (f32[48,16]{1,0:T(8,128)}, f32[48,16]{1,0:T(8,128)S(1)}, u32[]{:S(2)}) copy-start(f32[48,16]{1,0:T(8,128)S(1)} %broadcast_multiply_fusion) | copy-start | bytes 9220
  13.4 67.0 %copy-start.29 = (f32[768]{0:T(1024)}, f32[768]{0:T(1024)S(1)}, u32[]{:S(2)}) copy-start(f32[768]{0:T(1024)S(1)} %div.72) | copy-start | bytes 9220
  61.1 19.2 %copy-start.36 = (f32[768]{0:T(1024)}, f32[768]{0:T(1024)S(1)}, u32[]{:S(2)}) copy-start(f32[768]{0:T(1024)S(1)} %convert_element_type.156) | copy-start | bytes 9220
  61.2 19.2 %copy-start.27 = (f32[768]{0:T(1024)}, f32[768]{0:T(1024)S(1)}, u32[]{:S(2)}) copy-start(f32[768]{0:T(1024)S(1)} %convert_element_type.155) | copy-start | bytes 9220
  61.9 18.5 %copy-start.33 = (f32[768]{0:T(1024)}, f32[768]{0:T(1024)S(1)}, u32[]{:S(2)}) copy-start(f32[768]{0:T(1024)S(1)} %rsqrt.41) | copy-start | bytes 9220
  63.2 38.4 %copy-start.25 = (pred[48,16]{1,0:T(8,128)(4,1)}, pred[48,16]{1,0:T(8,128)(4,1)S(1)}, u32[]{:S(2)}) copy-start(pred[48,16]{1,0:T(8,128)(4,1)S(1)} %get-tuple-element.57) | copy-start | bytes 2308
  132.6 312.5 %copy-start.2 = (f32[768,768]{1,0:T(8,128)}, f32[768,768]{1,0:T(8,128)S(1)}, u32[]{:S(2)}) copy-start(f32[768,768]{1,0:T(8,128)S(1)} %get-tuple-element.61) | copy-start | bytes 7077892
  277.3 103.8 %all-gather.15.cloned.1.call-start = ((), (), s32[]{:S(2)}) async-start(), calls=%async_computation.8 | async-start | bytes 2654208 | tf_op jit(solution)/shard_map/all_gather | solution.py:146
  285.2 326.1 %reduce-scatter.7.cloned.1.call-start = ((), (), s32[]{:S(2)}) async-start(), calls=%async_computation.11 | async-start | bytes 2433024 | tf_op jit(solution)/shard_map/reduce_scatter | solution.py:245
  428.1 17.0 %slice-start.2 = ((s8[4718592]{0:T(1024)(128)(4,1)}), s8[4194304]{0:T(1024)(128)(4,1)S(1)}, s32[]{:S(2)}) async-start(s8[4718592]{0:T(1024)(128)(4,1)} %bitcast.106), calls=%async_computation.16 | async-start | bytes 8388608
  432.1 20.5 %copy-start.15 = (f32[48,768]{1,0:T(8,128)}, f32[48,768]{1,0:T(8,128)S(1)}, u32[]{:S(2)}) copy-start(f32[48,768]{1,0:T(8,128)S(1)} %add_add_fusion.4) | copy-start | bytes 442372
  432.3 12.8 %copy-start.18 = (bf16[768,768]{1,0:T(8,128)(2,1)}, bf16[768,768]{1,0:T(8,128)(2,1)S(1)}, u32[]{:S(2)}) copy-start(bf16[768,768]{1,0:T(8,128)(2,1)S(1)} %fusion.9) | copy-start | bytes 3538948
  432.3 12.8 %slice-start.3 = ((s8[4718592]{0:T(1024)(128)(4,1)}), s8[524288]{0:T(1024)(128)(4,1)S(1)}, s32[]{:S(2)}) async-start(s8[4718592]{0:T(1024)(128)(4,1)} %bitcast.106), calls=%async_computation.17 | async-start | bytes 1048576
  474.9 225.1 %reduce-scatter.5.cloned.1.call-start = ((), (), s32[]{:S(2)}) async-start(), calls=%async_computation.10 | async-start | bytes 7299072 | tf_op jit(solution)/shard_map/reduce_scatter | solution.py:244
  519.3 322.2 %reduce-scatter.9.cloned.1.call-start = ((), (), s32[]{:S(2)}) async-start(), calls=%async_computation.12 | async-start | bytes 9732096 | tf_op jit(solution)/shard_map/reduce_scatter | solution.py:203
  530.5 453.0 %reduce-scatter.11.cloned.1.call-start = ((), (), s32[]{:S(2)}) async-start(), calls=%async_computation.13 | async-start | bytes 9732096 | tf_op jit(solution)/shard_map/reduce_scatter | solution.py:205
  552.6 45.8 %copy-start.32 = (f32[768]{0:T(1024)S(1)}, f32[768]{0:T(1024)}, u32[]{:S(2)}) copy-start(f32[768]{0:T(1024)} %reshape.314) | copy-start | bytes 9220
  (42 other events, 141.4 us)
Sparse Core Ops, SparseCore 0:
  10.9 63.0 all-gather.6
  76.9 52.8 all-gather.8
  132.7 62.5 all-gather.10
  198.0 62.4 all-gather.12
  277.4 50.9 all-gather.16
  330.4 50.5 all-gather.14
  475.1 99.5 reduce-scatter.6
  581.9 118.1 reduce-scatter.4
  706.5 134.9 reduce-scatter.8
  848.9 134.5 reduce-scatter.10
where the time goes:
time: 996 us; the launch traced here: 992 us
  waiting for transfers between devices  585 us (59%)
  blocking collectives  139 us (14%)
  matrix products  131 us (13%)
  local copies, waits for them, and re-layouts  73.3 us (7%)
  other arithmetic  44.2 us (4%)
  between operations  18.8 us (2%)
    reduce_scatter x1, waiting for transfers between devices, on_device(): lax.psum_scatter(grad_wdown, ('dp', 'fsdp'), scatter_dimension=0, tiled=T...  142 us
    reduce_scatter x1, waiting for transfers between devices, on_device(): lax.psum_scatter(grad_wup, ('dp', 'fsdp'), scatter_dimension=0, tiled=True)  141 us
    reduce_scatter x1, waiting for transfers between devices, on_device(): lax.psum_scatter(grad_wqkv, ('dp', 'fsdp'), scatter_dimension=0, tiled=True)  88.8 us
    unnamed x2, blocking collectives  82.6 us
    all_gather x1, waiting for transfers between devices, on_device(): lax.all_gather(w_up, ('dp', 'fsdp'), axis=0, tiled=True)  61.4 us
    all_gather x1, waiting for transfers between devices, on_device(): image_piece = lax.all_gather(image_group, 'dp', axis=0, tiled=True)  48.4 us
    psum x1, blocking collectives, on_device(): objective = lax.psum(local_part, ('dp', 'fsdp'))  41.9 us
    all_gather x1, waiting for transfers between devices, on_device(): lax.all_gather(w_down, ('dp', 'fsdp'), axis=0, tiled=True)  37.2 us
  transfers between devices with their start and end apart: 10, of which 9 were waited for; matrix products, arithmetic and copies ran while one was open for 18% of the time, Pallas kernels for 0%

commit v1 on v0

v1 whole, which is shorter than its diff:
```python
import jax
import jax.numpy as jnp
from jax import lax
from jax.sharding import PartitionSpec as P

HEAD_DIM = 64
EPS = 1e-05
NORM_EPS = 1e-06
SCALE = 50.0
NEG = -1e30
AXES = ("dp", "fsdp")
F32 = jnp.float32
BF16 = jnp.bfloat16


def norm_stats(values):
    average = jnp.mean(values, axis=-1, keepdims=True)
    centred = values - average
    inverse = lax.rsqrt(jnp.mean(centred * centred, axis=-1, keepdims=True) + EPS)
    return centred * inverse, inverse


def norm_back(d_normed, hat, inverse, gain):
    d_hat = d_normed * gain
    mean_one = jnp.mean(d_hat, axis=-1, keepdims=True)
    mean_two = jnp.mean(d_hat * hat, axis=-1, keepdims=True)
    return inverse * (d_hat - mean_one - hat * mean_two)


def unit_scale(values):
    return lax.rsqrt(jnp.sum(values * values, axis=-1, keepdims=True) + NORM_EPS)


def dot(left, right, dims=((1,), (0,))):
    return lax.dot_general(left, right, (dims, ((), ())), preferred_element_type=F32)


def gelu_and_slope(upper):
    tail = lax.erfc(upper * (-(0.5**0.5)))
    half = 0.5 * tail
    slope = half + upper * jnp.exp(-0.5 * upper * upper) * (0.5 * jnp.pi) ** -0.5 * 0.5
    return upper * half, slope


def gather(value):
    return lax.all_gather(value, AXES, axis=0, tiled=True)


def scatter(value):
    return lax.psum_scatter(value, AXES, scatter_dimension=0, tiled=True)


def on_device(
    tokens,
    image_embed,
    counts,
    end_pos,
    ln1_gain,
    ln1_bias,
    w_qkv,
    w_out,
    ln2_gain,
    ln2_bias,
    w_up,
    b_up,
    w_down,
    b_down,
):
    caps, slots, dim = tokens.shape
    rows = caps * slots
    heads = dim // HEAD_DIM
    me = lax.axis_index(AXES)
    wqkv = gather(w_qkv)
    wout = gather(w_out)
    wup = gather(w_up)
    wdown = gather(w_down)
    small = [gather(v).astype(F32) for v in (ln1_gain, ln1_bias, ln2_gain, ln2_bias, b_up, b_down)]
    gain1, bias1, gain2, bias2, bup, bdown = small
    image = image_embed.astype(F32)
    image_low = (image * unit_scale(image)).astype(BF16)
    image_all = gather(image_low)

    lane_head = lax.broadcasted_iota(jnp.int32, (dim, heads), 0) // HEAD_DIM
    head_of = lax.broadcasted_iota(jnp.int32, (dim, heads), 1)
    pick = (lane_head == head_of).astype(BF16)

    def by_head(product):
        high = product.astype(BF16)
        low = (product - high.astype(F32)).astype(BF16)
        return dot(high, pick) + dot(low, pick)

    def spread(value):
        return dot(value, pick, ((1,), (1,)))

    positions = jnp.arange(slots, dtype=jnp.int32)
    at_end = (positions[None, :] == end_pos[:, None]).astype(F32)[:, :, None]
    counted = (positions[None, :] <= end_pos[:, None])[:, :, None]

    def row_at_end(value):
        return jnp.sum(value.reshape(caps, slots, -1) * at_end, axis=1)

    inputs = tokens.reshape(rows, dim).astype(F32)
    hat1, inverse1 = norm_stats(inputs)
    a1 = (hat1 * gain1 + bias1).astype(BF16)
    a1_end = row_at_end(a1.astype(F32)).astype(BF16)
    inputs_end = row_at_end(inputs)
    query = dot(a1_end, wqkv[:, :dim]).astype(BF16)
    kv = dot(a1, wqkv[:, dim:]).astype(BF16)
    keys = kv[:, :dim].reshape(caps, slots, dim).astype(F32)
    vals = kv[:, dim:].reshape(caps, slots, dim).astype(F32)
    query_f = query.astype(F32)[:, None, :]
    scores = by_head((query_f * keys).reshape(rows, dim)) * HEAD_DIM**-0.5
    scores = jnp.where(counted, scores.reshape(caps, slots, heads), NEG)
    top = jnp.max(scores, axis=1, keepdims=True)
    weight = jnp.exp(scores - top)
    probs = weight / jnp.sum(weight, axis=1, keepdims=True)
    probs_low = probs.astype(BF16)
    probs_wide = spread(probs_low.reshape(rows, heads)).reshape(caps, slots, dim)
    mixed = jnp.sum(probs_wide * vals, axis=1).astype(BF16)
    hidden1 = inputs_end + dot(mixed, wout)
    hat2, inverse2 = norm_stats(hidden1)
    a2 = (hat2 * gain2 + bias2).astype(BF16)
    upper = dot(a2, wup) + bup
    acted, slope = gelu_and_slope(upper)
    acted_low = acted.astype(BF16)
    pooled = hidden1 + dot(acted_low, wdown) + bdown
    scale_t = unit_scale(pooled)
    unit = pooled * scale_t
    text_low = unit.astype(BF16)
    own_image = image_low.astype(F32)
    diagonal = SCALE * jnp.sum(text_low.astype(F32) * own_image, axis=1)

    total = caps * counts.shape[0]
    slot_of = lax.broadcasted_iota(jnp.int32, (counts.shape[0], caps), 1)
    valid_all = (slot_of < counts[:, None]).astype(F32).reshape(total)
    own_count = jnp.sum(jnp.where(jnp.arange(counts.shape[0]) == me, counts, 0))
    own_valid = (jnp.arange(caps) < own_count).astype(F32)
    growth = jnp.exp(SCALE * dot(text_low, image_all, ((1,), (1,))))
    row_sum = jnp.sum(growth * valid_all[None, :], axis=1)
    col_sum = lax.psum(jnp.sum(growth * own_valid[:, None], axis=0), AXES)
    row_part = jnp.sum(own_valid * (0.5 * jnp.log(row_sum) - diagonal))
    objective = lax.psum(row_part, AXES) + 0.5 * jnp.sum(valid_all * jnp.log(col_sum))
    mean_loss = objective / jnp.sum(counts).astype(F32)
    inverse_sum = 1.0 / row_sum[:, None] + 1.0 / col_sum[None, :]
    coef = 0.5 * SCALE * growth * inverse_sum * (own_valid[:, None] * valid_all[None, :])
    d_text = dot(coef.astype(BF16), image_all) - SCALE * own_valid[:, None] * own_image
    d_pooled = (d_text - unit * jnp.sum(unit * d_text, axis=-1, keepdims=True)) * scale_t

    dm = d_pooled.astype(BF16)
    g_wdown = dot(acted_low, dm, ((0,), (0,)))
    g_bdown = jnp.sum(dm.astype(F32), axis=0)
    du = (dot(dm, wdown, ((1,), (1,))) * slope).astype(BF16)
    g_bup = jnp.sum(du.astype(F32), axis=0)
    g_wup = dot(a2, du, ((0,), (0,)))
    d_a2 = dot(du, wup, ((1,), (1,)))
    g_gain2 = jnp.sum(d_a2 * hat2, axis=0)
    g_bias2 = jnp.sum(d_a2, axis=0)
    d_hidden1 = d_pooled + norm_back(d_a2, hat2, inverse2, gain2)
    da = d_hidden1.astype(BF16)
    g_wout = dot(mixed, da, ((0,), (0,)))
    d_mixed = dot(da, wout, ((1,), (1,))).astype(BF16).astype(F32)[:, None, :]
    d_vals = probs_wide * d_mixed
    d_probs = by_head((vals * d_mixed).reshape(rows, dim)).reshape(caps, slots, heads)
    d_scores = probs * (d_probs - jnp.sum(d_probs * probs, axis=1, keepdims=True))
    d_wide = spread(d_scores.astype(BF16).reshape(rows, heads)).reshape(caps, slots, dim)
    d_query = (HEAD_DIM**-0.5 * jnp.sum(d_wide * keys, axis=1)).astype(BF16)
    d_keys = HEAD_DIM**-0.5 * d_wide * query_f
    d_kv = jnp.concatenate([d_keys, d_vals], axis=-1).reshape(rows, 2 * dim).astype(BF16)
    g_wqkv = jnp.concatenate(
        [dot(a1_end, d_query, ((0,), (0,))), dot(a1, d_kv, ((0,), (0,)))], axis=1
    )
    d_a1_end = dot(d_query, wqkv[:, :dim], ((1,), (1,)))
    d_a1 = dot(d_kv, wqkv[:, dim:], ((1,), (1,)))
    d_a1 = d_a1 + (d_a1_end[:, None, :] * at_end).reshape(rows, dim)
    g_gain1 = jnp.sum(d_a1 * hat1, axis=0)
    g_bias1 = jnp.sum(d_a1, axis=0)
    grad_tokens = norm_back(d_a1, hat1, inverse1, gain1).reshape(caps, slots, dim)
    grad_tokens = grad_tokens + at_end * d_hidden1[:, None, :]
    return (
        mean_loss,
        grad_tokens,
        scatter(g_gain1),
        scatter(g_bias1),
        scatter(g_wqkv),
        scatter(g_wout),
        scatter(g_gain2),
        scatter(g_bias2),
        scatter(g_wup),
        scatter(g_bup),
        scatter(g_wdown),
        scatter(g_bdown),
    )


def solution(mesh):
    one, two, three = P(AXES), P(AXES, None), P(AXES, None, None)
    placed = (three, two, P(), one, one, one, two, two, one, one, two, one, two, one)
    given = (P(), three, one, one, two, two, one, one, two, one, two, one)
    return jax.shard_map(
        on_device, mesh=mesh, in_specs=placed, out_specs=given, check_vma=False
    )
```

time: 996 us -> 918 us (0.922)
  matrix products: 131 us -> 63.6 us
  waiting for transfers between devices: 585 us -> 636 us
  local copies, waits for them, and re-layouts: 73.3 us -> 32.1 us
  blocking collectives: 139 us -> 124 us
    dot_general x21 -> x23, matrix products: 131 us -> 63.6 us  [dot(): lax.dot_general(left, right, (dims, ((), ())), preferred_element_type=F32)]
    reduce_scatter x4, waiting for transfers between devices: 372 us -> 423 us  [scatter(): return lax.psum_scatter(value, AXES, scatter_dimension=0, tiled=True)]
    unnamed x2 -> x1, blocking collectives: 82.6 us -> 42.6 us
    psum x1 -> x2, blocking collectives: 41.9 us -> 81.9 us  [the longest x1 43 us: on_device(): lax.psum(row_part, AXES) + 0.5 * jnp.sum(valid_all * jnp.log(col_sum))]
    convert_element_type x5 -> x1, local copies, waits for them, and re-layouts: 29.9 us -> 0.97 us  [on_device(): at_end = (positions[None, :] == end_pos[:, None]).astype(F32)[:, :, None]]
    all_gather x2 -> x0, blocking collectives: 14.3 us -> none  [the longest x1 7.87 us: on_device(): lax.all_gather(image_low, 'fsdp', axis=0, tiled=True)]
    reshape x2, local copies, waits for them, and re-layouts: 16.4 us -> 3.29 us  [the longest x1 1.65 us: on_device(): scores = jnp.where(counted, scores.reshape(caps, slots, heads), NEG)]
    unnamed x130 -> x146, local copies, waits for them, and re-layouts: 21.4 us -> 16.2 us
  transfers between devices with their start and end apart: 10 -> 9, of which waited for: 9 -> 9; matrix products, arithmetic and copies ran while one was open for 18% -> 10% of each run, Pallas kernels for 0% -> 0%
where the time goes in v1:
time: 918 us; the launch traced here: 916 us
  waiting for transfers between devices  636 us (69%)
  blocking collectives  124 us (14%)
  matrix products  63.6 us (7%)
  other arithmetic  41.9 us (5%)
  local copies, waits for them, and re-layouts  32.1 us (3%)
  between operations  17.5 us (2%)
    reduce_scatter x4, waiting for transfers between devices, scatter(): return lax.psum_scatter(value, AXES, scatter_dimension=0, tiled=True)  423 us
    all_gather x5, waiting for transfers between devices, gather(): return lax.all_gather(value, AXES, axis=0, tiled=True)  210 us
    dot_general x23, matrix products, dot(): lax.dot_general(left, right, (dims, ((), ())), preferred_element_type=F32)  63.6 us
    psum x1, blocking collectives, on_device(): lax.psum(row_part, AXES) + 0.5 * jnp.sum(valid_all * jnp.log(col_sum))  43 us
    unnamed x1, blocking collectives  42.6 us
    psum x1, blocking collectives, on_device(): col_sum = lax.psum(jnp.sum(growth * own_valid[:, None], axis=0), AXES)  38.9 us
  transfers between devices with their start and end apart: 9, of which 9 were waited for; matrix products, arithmetic and copies ran while one was open for 10% of the time, Pallas kernels for 0%

profile of v1, /device:TPU:0, one launch (start us, length us, event | category | flops | bytes accessed | tf_op | source)
XLA Modules:
  0.0 916.0 jit_solution(16003261855563957227)
XLA Ops:
  17.0 42.6 %all-reduce.13 = (bf16[768]{0:T(1024)(128)(2,1)S(1)}, bf16[768]{0:T(1024)(128)(2,1)S(1)}, bf16[768]{0:T(1024)(128)(2,1)S(1)}, bf16[3072]{0:T(1024)(128)(2,1)S(1)...) all-reduce(bf16[768]{0:T(1024)(128)(2,1)S(1)} %dynamic-update-slice, ...), channel_id=1, replica_groups=mesh['dp'=8,'fsdp'=4] {'dp','fsdp'}, use_global_device_ids=true, to_apply=%add.1 | all-reduce | flops 6912 | bytes 27648
  69.0 4.8 all-gather.6.cloned.1.call-done
  76.1 4.0 convolution_convert_fusion
  100.8 28.9 %all-gather.8.cloned.1.call-done = bf16[768,768]{1,0:T(8,128)(2,1)} async-done(((bf16[24,768]{1,0:T(8,128)(2,1)}), bf16[768,768]{1,0:T(8,128)(2,1)}) %all-gather.8.cloned.1.call-update) | async-done | bytes 1179664 | tf_op jit(solution)/shard_map/all_gather | solution.py:46
  132.8 62.4 %all-gather.10.cloned.1.call-done = bf16[768,3072]{1,0:T(8,128)(2,1)} async-done(((bf16[24,3072]{1,0:T(8,128)(2,1)}), bf16[768,3072]{1,0:T(8,128)(2,1)}) %all-gather.10.cloned.1.call-update) | async-done | bytes 4718608 | tf_op jit(solution)/shard_map/all_gather | solution.py:46
  195.2 4.2 convolution_add_fusion
  199.4 61.1 %all-gather.12.cloned.1.call-done = bf16[3072,768]{1,0:T(8,128)(2,1)} async-done(((bf16[96,768]{1,0:T(8,128)(2,1)}), bf16[3072,768]{1,0:T(8,128)(2,1)}) %all-gather.12.cloned.1.call-update) | async-done | bytes 4718608 | tf_op jit(solution)/shard_map/all_gather | solution.py:46
  260.5 5.1 multiply_reduce_fusion.14
  266.1 53.2 %all-gather.14.cloned.1.call-done = bf16[1536,768]{1,0:T(8,128)(2,1)} async-done(((bf16[48,768]{1,0:T(8,128)(2,1)}), bf16[1536,768]{1,0:T(8,128)(2,1)}) %all-gather.14.cloned.1.call-update) | async-done | bytes 2359312 | tf_op jit(solution)/shard_map/all_gather | solution.py:46
  319.3 4.0 multiply_reduce_fusion.9
  323.3 38.9 %psum.15 = f32[1536]{0:T(1024)} all-reduce(f32[1536]{0:T(1024)} %get-tuple-element.20), channel_id=1, replica_groups=mesh['dp'=8,'fsdp'=4] {'dp','fsdp'}, use_global_device_ids=true, to_apply=%region_17.18 | all-reduce | flops 1536 | bytes 12288 | tf_op jit(solution)/shard_map/psum | solution.py:140
  364.2 3.1 multiply_reduce_fusion.13
  368.1 5.2 convert_reduce_fusion.1
  383.6 4.7 fusion
  399.6 4.0 convolution_bitcast_fusion
  403.6 3.4 pad_maximum_fusion
  408.0 5.1 fusion.90
  414.2 6.2 fusion.83
  426.0 3.2 multiply_reduce_fusion
  430.4 43.0 %all-reduce.12 = (f32[]{:T(128)}, f32[768]{0:T(1024)}, f32[768]{0:T(1024)}, f32[768]{0:T(1024)}, f32[768]{0:T(1024)}, /*index=5*/f32[3072]{0:T(1024)}, f32[768]{0:T(1024)S(1)}) all-reduce(f32[]{:T(128)} %select_reduce_fusion.2, f32[768]{0:T(1024)} %get-tuple-element.12, ...), channel_id=1, replica_groups=mesh['dp'=8,'fsdp'=4] {'dp','fsdp'}, use_global_device_ids=true, to_apply=%region_15.16 | all-reduce | flops 6913 | bytes 55304 | tf_op jit(solution)/shard_map/psum | solution.py:142
  485.6 13.8 %reduce-scatter.7.cloned.1.call-done = f32[24,768]{1,0:T(8,128)} async-done(((f32[768,768]{1,0:T(8,128)}), f32[24,768]{1,0:T(8,128)}) %reduce-scatter.7.cloned.1.call-update) | async-done | bytes 73744 | tf_op jit(solution)/shard_map/reduce_scatter | solution.py:50
  499.4 125.5 %reduce-scatter.5.cloned.1.call-done = f32[24,2304]{1,0:T(8,128)} async-done(((f32[768,2304]{1,0:T(8,128)}), f32[24,2304]{1,0:T(8,128)}) %reduce-scatter.5.cloned.1.call-update) | async-done | bytes 221200 | tf_op jit(solution)/shard_map/reduce_scatter | solution.py:50
  624.8 141.2 %reduce-scatter.9.cloned.1.call-done = f32[24,3072]{1,0:T(8,128)} async-done(((f32[768,3072]{1,0:T(8,128)}), f32[24,3072]{1,0:T(8,128)}) %reduce-scatter.9.cloned.1.call-update) | async-done | bytes 294928 | tf_op jit(solution)/shard_map/reduce_scatter | solution.py:50
  766.0 142.3 %reduce-scatter.11.cloned.1.call-done = f32[96,768]{1,0:T(8,128)} async-done(((f32[3072,768]{1,0:T(8,128)}), f32[96,768]{1,0:T(8,128)}) %reduce-scatter.11.cloned.1.call-update) | async-done | bytes 294928 | tf_op jit(solution)/shard_map/reduce_scatter | solution.py:50
  (240 shorter events, 88.7 us)
Async XLA Ops:
  7.2 9.0 copy-start.59
  7.2 9.2 %copy-start.60 = (bf16[24]{0:T(256)(128)(2,1)S(1)}, bf16[24]{0:T(256)(128)(2,1)}, u32[]{:S(2)}) copy-start(bf16[24]{0:T(256)(128)(2,1)} %param.22) | copy-start | bytes 148
  7.3 9.5 %copy-start.61 = (bf16[96]{0:T(256)(128)(2,1)S(1)}, bf16[96]{0:T(256)(128)(2,1)}, u32[]{:S(2)}) copy-start(bf16[96]{0:T(256)(128)(2,1)} %param.25) | copy-start | bytes 580
  7.3 52.4 %copy-start.53 = (s32[32]{0:T(128)S(1)}, s32[32]{0:T(128)}, u32[]{:S(2)}) copy-start(s32[32]{0:T(128)} %param.16) | copy-start | bytes 388
  7.3 66.5 %all-gather.6.cloned.1.call-start = ((), (), s32[]{:S(2)}) async-start(), calls=%async_computation.4 | async-start | bytes 3649536 | tf_op jit(solution)/shard_map/all_gather | solution.py:46
  8.0 121.7 %all-gather.8.cloned.1.call-start = ((), (), s32[]{:S(2)}) async-start(), calls=%async_computation.5 | async-start | bytes 1216512 | tf_op jit(solution)/shard_map/all_gather | solution.py:46
  8.8 186.5 %all-gather.10.cloned.1.call-start = ((), (), s32[]{:S(2)}) async-start(), calls=%async_computation.6 | async-start | bytes 4866048 | tf_op jit(solution)/shard_map/all_gather | solution.py:46
  9.5 251.0 %all-gather.12.cloned.1.call-start = ((), (), s32[]{:S(2)}) async-start(), calls=%async_computation.7 | async-start | bytes 4866048 | tf_op jit(solution)/shard_map/all_gather | solution.py:46
  10.1 309.2 %all-gather.14.cloned.1.call-start = ((), (), s32[]{:S(2)}) async-start(), calls=%async_computation.8 | async-start | bytes 2433024 | tf_op jit(solution)/shard_map/all_gather | solution.py:46
  12.7 486.6 %reduce-scatter.7.cloned.1.call-start = ((), (), s32[]{:S(2)}) async-start(), calls=%async_computation.10 | async-start | bytes 2433024 | tf_op jit(solution)/shard_map/reduce_scatter | solution.py:50
  14.3 50.9 %copy-start.28 = (f32[48,16]{1,0:T(8,128)}, f32[48,16]{1,0:T(8,128)S(1)}, u32[]{:S(2)}) copy-start(f32[48,16]{1,0:T(8,128)S(1)} %broadcast_multiply_fusion.3) | copy-start | bytes 9220
  14.9 59.0 %copy-start.34 = (f32[768]{0:T(1024)}, f32[768]{0:T(1024)S(1)}, u32[]{:S(2)}) copy-start(f32[768]{0:T(1024)S(1)} %div.82) | copy-start | bytes 9220
  15.5 58.3 %copy-start.26 = (f32[48,16]{1,0:T(8,128)}, f32[48,16]{1,0:T(8,128)S(1)}, u32[]{:S(2)}) copy-start(f32[48,16]{1,0:T(8,128)S(1)} %get-tuple-element.54) | copy-start | bytes 9220
  15.5 58.3 %copy-start.32 = (pred[48,16]{1,0:T(8,128)(4,1)}, pred[48,16]{1,0:T(8,128)(4,1)S(1)}, u32[]{:S(2)}) copy-start(pred[48,16]{1,0:T(8,128)(4,1)S(1)} %get-tuple-element.53) | copy-start | bytes 2308
  59.5 14.3 %copy-start.38 = (f32[768]{0:T(1024)}, f32[768]{0:T(1024)S(1)}, u32[]{:S(2)}) copy-start(f32[768]{0:T(1024)S(1)} %convert_element_type.192) | copy-start | bytes 9220
  59.5 14.3 %copy-start.30 = (f32[768]{0:T(1024)}, f32[768]{0:T(1024)S(1)}, u32[]{:S(2)}) copy-start(f32[768]{0:T(1024)S(1)} %convert_element_type.191) | copy-start | bytes 9220
  59.6 14.3 %copy-start.29 = (f32[48,16]{1,0:T(8,128)}, f32[48,16]{1,0:T(8,128)S(1)}, u32[]{:S(2)}) copy-start(f32[48,16]{1,0:T(8,128)S(1)} %add_rsqrt_fusion) | copy-start | bytes 9220
  59.7 14.2 %copy-start.36 = (f32[768]{0:T(1024)}, f32[768]{0:T(1024)S(1)}, u32[]{:S(2)}) copy-start(f32[768]{0:T(1024)S(1)} %rsqrt.37) | copy-start | bytes 9220
  63.7 10.1 %copy-start.18 = (bf16[48,768]{1,0:T(8,128)(2,1)}, bf16[48,768]{1,0:T(8,128)(2,1)S(1)}, u32[]{:S(2)}) copy-start(bf16[48,768]{1,0:T(8,128)(2,1)S(1)} %get-tuple-element.16) | copy-start | bytes 221188
  364.2 9.1 slice-start
  380.4 12.7 %copy-start.2 = (f32[48,16,768]{2,1,0:T(8,128)S(1)}, f32[48,16,768]{2,1,0:T(8,128)}, u32[]{:S(2)}) copy-start(f32[48,16,768]{2,1,0:T(8,128)} %get-tuple-element.56) | copy-start | bytes 7077892
  399.4 225.4 %reduce-scatter.5.cloned.1.call-start = ((), (), s32[]{:S(2)}) async-start(), calls=%async_computation.9 | async-start | bytes 7299072 | tf_op jit(solution)/shard_map/reduce_scatter | solution.py:50
  407.0 359.1 %reduce-scatter.9.cloned.1.call-start = ((), (), s32[]{:S(2)}) async-start(), calls=%async_computation.11 | async-start | bytes 9732096 | tf_op jit(solution)/shard_map/reduce_scatter | solution.py:50
  413.1 495.2 %reduce-scatter.11.cloned.1.call-start = ((), (), s32[]{:S(2)}) async-start(), calls=%async_computation.12 | async-start | bytes 9732096 | tf_op jit(solution)/shard_map/reduce_scatter | solution.py:50
  (49 other events, 146.8 us)
Sparse Core Ops, SparseCore 0:
  11.0 62.7 all-gather.5
  76.7 52.9 all-gather.7
  132.6 62.5 all-gather.9
  198.0 62.4 all-gather.11
  263.2 56.0 all-gather.13
  399.5 99.7 reduce-scatter.6
  506.6 118.2 reduce-scatter.4
  631.3 134.6 reduce-scatter.8
  773.5 134.7 reduce-scatter.10
